TPU v7x, 128 devices: a whole 4x4x4 slice. The times are simulated.
128 devices in a mesh: room: 4 (over x_hi, core), geom: 32 (over z, x_lo, y).
Axes of the slice: x: 4 (x_hi: 2, x_lo: 2; x = x_hi * 2 + x_lo), y: 4, z: 4, core: 2. Of those that a mesh axis runs over, the one named last changes fastest.
Arguments:
- queries: bfloat16 [4, 4096, 512], P('room', 'geom'), may hold values from -6 to 6
- features: bfloat16 [4, 4096, 512], P('room', 'geom'), may hold values from -45 to 45
- visible: int32 [4, 32, 32], P('room', 'geom'), may hold values from 0 to 1, as said below
- cotangent: bfloat16 [4, 4096, 512], P('room', 'geom'), may hold values from -0.125 to 0.125
- w_query: bfloat16 [512, 512], replicated, may hold values from -0.25 to 0.25
- w_key: bfloat16 [512, 512], replicated, may hold values from -0.25 to 0.25
- w_value: bfloat16 [512, 512], replicated, may hold values from -0.25 to 0.25
- w_out: bfloat16 [512, 512], replicated, may hold values from -0.25 to 0.25
- w_up: bfloat16 [512, 1024], replicated, may hold values from -0.25 to 0.25
- w_down: bfloat16 [1024, 512], replicated, may hold values from -0.1875 to 0.1875
- gain_attn: float32 [512], replicated, may hold values from 0.25 to 1.75
- gain_mlp: float32 [512], replicated, may hold values from 0.25 to 1.75
Outputs:
- output: bfloat16 [4, 4096, 512], P('room', 'geom')
- grad_query_w: bfloat16 [512, 512], replicated
- grad_key_w: bfloat16 [512, 512], replicated
- grad_value_w: bfloat16 [512, 512], replicated
- grad_out_w: bfloat16 [512, 512], replicated
- grad_up_w: bfloat16 [512, 1024], replicated
- grad_down_w: bfloat16 [1024, 512], replicated
- grad_gain_attn: bfloat16 [512], replicated
- grad_gain_mlp: bfloat16 [512], replicated
Inputs may be any that keep to these rules, and one draw needn't show every extreme that they name: `visible`: every query block sees at least one key block.
All inputs are finite; a program needn't handle non-finite values.
Results may differ from a plain program's by a relative error of at most 0.017.
The roundings to bfloat16 on the way count: a program that leaves them out, or rounds other values in their place, can miss the bound.
Values may be sent and summed in bfloat16 or wider, within the bound.
No kernel may reach another device: no remote copies, remote signals or barrier semaphores. Data moves between devices by JAX's collectives and lax.ppermute only.
A program may use at most 128 MiB of HBM per device.

v0:
```python
import math
import jax
import jax.numpy as jnp
from jax import lax
from jax.sharding import PartitionSpec as P

HEADS = 4
BLK = 128
EPSILON = 1e-05
GELU_COEF = math.sqrt(2.0 / math.pi)


def normalize(inputs, gain):
    center = inputs - jnp.mean(inputs, axis=-1, keepdims=True)
    inverse = lax.rsqrt(jnp.mean(center * center, axis=-1, keepdims=True) + EPSILON)
    scaled = center * inverse
    return (scaled, inverse, scaled * gain)


def gelu_pair(inputs):
    inner = GELU_COEF * (inputs + 0.044715 * inputs * inputs * inputs)
    tangent = jnp.tanh(inner)
    value = 0.5 * inputs * (1.0 + tangent)
    slope = 0.5 * (1.0 + tangent) + 0.5 * inputs * (1.0 - tangent * tangent) * GELU_COEF * (
        1.0 + 3.0 * 0.044715 * inputs * inputs
    )
    return (value, slope)


def mult_nt(left, right):
    return lax.dot_general(
        left, right, (((1,), (1,)), ((), ())), preferred_element_type=jnp.float32
    )


def mult_tn(left, right):
    return lax.dot_general(
        left, right, (((0,), (0,)), ((), ())), preferred_element_type=jnp.float32
    )


def device_step(
    queries,
    visible,
    cotangent,
    key_rows,
    value_rows,
    w_query,
    w_out,
    w_up,
    w_down,
    gain_attn,
    gain_mlp,
):
    head_size = key_rows.shape[1] // HEADS
    factor = 1.0 / math.sqrt(head_size)
    allowed = jnp.repeat(jnp.repeat(visible > 0, BLK, axis=0), BLK, axis=1)
    inputs = queries.astype(jnp.float32)
    scaled_one, inverse_one, normed = normalize(inputs, gain_attn)
    normed_b = normed.astype(jnp.bfloat16)
    query_rows = jnp.dot(normed_b, w_query, preferred_element_type=jnp.float32).astype(jnp.bfloat16)
    contexts = []
    saved = []
    for head_index in range(HEADS):
        lower = head_index * head_size
        query_head = query_rows[:, lower : lower + head_size]
        key_head = key_rows[:, lower : lower + head_size]
        value_head = value_rows[:, lower : lower + head_size]
        scores = mult_nt(query_head, key_head) * factor
        scores = jnp.where(allowed, scores, -1e30)
        highest = jnp.max(scores, axis=-1, keepdims=True)
        expo = jnp.exp(scores - highest)
        attend = expo / jnp.sum(expo, axis=-1, keepdims=True)
        attend_b = attend.astype(jnp.bfloat16)
        contexts.append(
            jnp.dot(attend_b, value_head, preferred_element_type=jnp.float32).astype(jnp.bfloat16)
        )
        saved.append((attend, attend_b))
    context = jnp.concatenate(contexts, axis=1)
    mixed = inputs + jnp.dot(context, w_out, preferred_element_type=jnp.float32)
    scaled_two, inverse_two, normed_two = normalize(mixed, gain_mlp)
    normed_two_b = normed_two.astype(jnp.bfloat16)
    upper = jnp.dot(normed_two_b, w_up, preferred_element_type=jnp.float32)
    activated, slope = gelu_pair(upper)
    activated_b = activated.astype(jnp.bfloat16)
    output = (mixed + jnp.dot(activated_b, w_down, preferred_element_type=jnp.float32)).astype(
        jnp.bfloat16
    )
    grad_down = mult_tn(activated_b, cotangent)
    grad_activated = mult_nt(cotangent, w_down)
    grad_upper_b = (grad_activated * slope).astype(jnp.bfloat16)
    grad_up = mult_tn(normed_two_b, grad_upper_b)
    grad_normed_two = mult_nt(grad_upper_b, w_up)
    grad_gain_mlp = jnp.sum(grad_normed_two * scaled_two, axis=0)
    grad_scaled = grad_normed_two * gain_mlp
    mean_one = jnp.mean(grad_scaled, axis=-1, keepdims=True)
    mean_two = jnp.mean(grad_scaled * scaled_two, axis=-1, keepdims=True)
    grad_mixed = cotangent.astype(jnp.float32) + inverse_two * (
        grad_scaled - mean_one - scaled_two * mean_two
    )
    grad_mixed_b = grad_mixed.astype(jnp.bfloat16)
    grad_out = mult_tn(context, grad_mixed_b)
    grad_context = mult_nt(grad_mixed_b, w_out).astype(jnp.bfloat16)
    grad_queries = []
    grad_keys = []
    grad_values = []
    for head_index in range(HEADS):
        lower = head_index * head_size
        query_head = query_rows[:, lower : lower + head_size]
        key_head = key_rows[:, lower : lower + head_size]
        value_head = value_rows[:, lower : lower + head_size]
        attend, attend_b = saved[head_index]
        grad_head = grad_context[:, lower : lower + head_size]
        grad_attend = mult_nt(grad_head, value_head)
        grad_values.append(mult_tn(attend_b, grad_head))
        centre = jnp.sum(attend * grad_attend, axis=-1, keepdims=True)
        grad_scores = (attend * (grad_attend - centre) * factor).astype(jnp.bfloat16)
        grad_queries.append(jnp.dot(grad_scores, key_head, preferred_element_type=jnp.float32))
        grad_keys.append(mult_tn(grad_scores, query_head))
    grad_query_rows = jnp.concatenate(grad_queries, axis=1).astype(jnp.bfloat16)
    partial_keys = jnp.concatenate(grad_keys, axis=1).astype(jnp.bfloat16)
    partial_values = jnp.concatenate(grad_values, axis=1).astype(jnp.bfloat16)
    grad_query = mult_tn(normed_b, grad_query_rows)
    grad_normed = mult_nt(grad_query_rows, w_query)
    grad_gain_attn = jnp.sum(grad_normed * scaled_one, axis=0)
    grads = (grad_query, grad_out, grad_up, grad_down, grad_gain_attn, grad_gain_mlp)
    return (output, grads, partial_keys, partial_values)


def local(
    queries,
    features,
    visible,
    cotangent,
    w_query,
    w_key,
    w_value,
    w_out,
    w_up,
    w_down,
    gain_attn,
    gain_mlp,
):
    local_feat = features[0]
    local_keys = jnp.dot(local_feat, w_key, preferred_element_type=jnp.float32).astype(jnp.bfloat16)
    local_values = jnp.dot(local_feat, w_value, preferred_element_type=jnp.float32).astype(
        jnp.bfloat16
    )
    key_rows, value_rows = (
        lax.all_gather(local_keys, "geom", axis=0, tiled=True),
        lax.all_gather(local_values, "geom", axis=0, tiled=True),
    )
    output, grads, partial_keys, partial_values = device_step(
        queries[0],
        visible[0],
        cotangent[0],
        key_rows,
        value_rows,
        w_query,
        w_out,
        w_up,
        w_down,
        gain_attn,
        gain_mlp,
    )
    key_sum, value_sum = (
        lax.psum_scatter(partial_keys.astype(jnp.float32), "geom", scatter_dimension=0, tiled=True),
        lax.psum_scatter(
            partial_values.astype(jnp.float32), "geom", scatter_dimension=0, tiled=True
        ),
    )
    feat_float = local_feat.astype(jnp.float32)
    grad_key = lax.dot_general(
        feat_float,
        key_sum,
        (((0,), (0,)), ((), ())),
        precision=lax.Precision.HIGHEST,
        preferred_element_type=jnp.float32,
    )
    grad_value = lax.dot_general(
        feat_float,
        value_sum,
        (((0,), (0,)), ((), ())),
        precision=lax.Precision.HIGHEST,
        preferred_element_type=jnp.float32,
    )
    grad_query, grad_out, grad_up, grad_down, grad_gain_attn, grad_gain_mlp = grads
    totals = lax.psum(
        (
            grad_query,
            grad_key,
            grad_value,
            grad_out,
            grad_up,
            grad_down,
            grad_gain_attn,
            grad_gain_mlp,
        ),
        ("room", "geom"),
    )
    summed = [piece.astype(jnp.bfloat16) for piece in totals]
    return (
        output[None],
        summed[0],
        summed[1],
        summed[2],
        summed[3],
        summed[4],
        summed[5],
        summed[6],
        summed[7],
    )


def solution(mesh):
    placed = (
        P("room", "geom", None),
        P("room", "geom", None),
        P("room", "geom", None),
        P("room", "geom", None),
        P(),
        P(),
        P(),
        P(),
        P(),
        P(),
        P(),
        P(),
    )
    return jax.shard_map(
        local,
        mesh=mesh,
        in_specs=placed,
        out_specs=(P("room", "geom", None), P(), P(), P(), P(), P(), P(), P(), P()),
        check_vma=False,
    )
```

profile of v0, /device:TPU:0, one launch (start us, length us, event | category | flops | bytes accessed | tf_op | source)
XLA Modules:
  0.0 832.1 jit_solution(216690923784676051)
XLA Ops:
  7.3 2.1 convolution_convert_fusion.10
  9.5 2.0 convolution_convert_fusion.9
  11.5 1.0 convert_reduce_fusion
  12.6 1.1 fusion.54
  14.1 156.3 %all-gather.3.cloned.1.call-done = bf16[4096,512]{1,0:T(8,128)(2,1)} async-done(((bf16[128,512]{1,0:T(8,128)(2,1)}), bf16[4096,512]{1,0:T(8,128)(2,1)}) %all-gather.3.cloned.1.call-update) | async-done | bytes 4194320 | tf_op jit(solution)/shard_map/all_gather | solution.py:150
  170.4 1.9 fusion.99
  172.3 1.4 copy-done.8
  173.7 0.4 fusion.5
  174.2 0.6 fusion.98
  174.7 1.3 copy-done.5
  176.0 0.4 fusion.7
  176.4 0.5 fusion.97
  177.0 0.4 fusion.9
  177.5 0.5 fusion.96
  178.3 0.4 fusion.11
  178.8 151.2 %all-gather.5.cloned.1.call-done = bf16[4096,512]{1,0:T(8,128)(2,1)} async-done(((bf16[128,512]{1,0:T(8,128)(2,1)}), bf16[4096,512]{1,0:T(8,128)(2,1)}) %all-gather.5.cloned.1.call-update) | async-done | bytes 4194320 | tf_op jit(solution)/shard_map/all_gather | solution.py:151
  329.9 2.7 convolution_convert_fusion.19
  332.7 1.0 copy-done.78
  333.7 0.7 convolution_convert_fusion.18
  334.5 0.8 copy-done.3
  335.3 0.7 convolution_convert_fusion.17
  336.1 0.7 convolution_convert_fusion.16
  338.5 0.6 fusion.12
  339.1 1.1 multiply_reduce_fusion.4
  340.7 0.6 convolution_convert_fusion.2
  341.4 1.0 copy-done.9
  342.4 0.6 convolution_convert_fusion.3
  343.0 0.6 convolution_convert_fusion.1
  343.7 0.6 convolution_convert_fusion
  344.3 3.6 maximum_convert_fusion.1
  348.6 2.7 multiply_reduce_fusion.3
  351.3 0.7 multiply_convert_fusion.3
  352.2 0.5 convolution_convert_fusion.7
  352.7 0.9 copy-done.79
  353.7 0.9 copy-done.7
  354.5 0.7 multiply_reduce_fusion.2
  355.2 0.7 multiply_convert_fusion.2
  356.0 0.5 convolution_convert_fusion.6
  356.4 1.5 copy-done.4
  357.9 0.7 multiply_reduce_fusion.1
  358.6 0.7 multiply_convert_fusion.1
  359.4 0.5 convolution_convert_fusion.5
  360.1 0.7 multiply_reduce_fusion
  360.8 0.7 multiply_convert_fusion
  361.5 1.0 copy-done.17
  362.4 0.5 convolution_convert_fusion.4
  362.9 3.9 maximum_convert_fusion
  366.8 1.9 convolution_convert_fusion.15
  368.8 2.1 convolution_convert_fusion.14
  370.9 0.6 convolution_convert_fusion.13
  371.5 0.6 convolution_convert_fusion.12
  372.1 0.9 fusion.14
  373.0 0.5 fusion.86
  373.6 1.3 fusion.79
  374.9 1.4 fusion.78
  376.3 1.9 fusion.55
  378.1 1.0 fusion.15
  379.2 147.8 %reduce-scatter.5.cloned.1.call-done = f32[128,512]{1,0:T(8,128)} async-done(((f32[4096,512]{1,0:T(8,128)}), f32[128,512]{1,0:T(8,128)}) %reduce-scatter.5.cloned.1.call-update) | async-done | bytes 262160 | tf_op jit(solution)/shard_map/reduce_scatter | solution.py:168
  526.9 2.5 convolution_bitcast_fusion
  529.5 174.9 %reduce-scatter.3.cloned.1.call-done = f32[128,512]{1,0:T(8,128)} async-done(((f32[4096,512]{1,0:T(8,128)}), f32[128,512]{1,0:T(8,128)}) %reduce-scatter.3.cloned.1.call-update) | async-done | bytes 262160 | tf_op jit(solution)/shard_map/reduce_scatter | solution.py:167
  704.4 2.6 convolution_bitcast_fusion.1
  707.0 114.5 %all-reduce.2 = (bf16[512,512]{1,0:T(8,128)(2,1)}, bf16[512,512]{0,1:T(8,128)(2,1)}, bf16[512,512]{0,1:T(8,128)(2,1)}, bf16[512,512]{1,0:T(8,128)(2,1)}, bf16[51...) all-reduce(f32[512,512]{1,0:T(8,128)} %fusion.78, ...), channel_id=1, replica_groups=mesh['room'=4,'geom'=32] {'room','geom'}, use_global_device_ids=true, to_apply=%region_18.19 | all-reduce | flops 2098176 | bytes 12589056 | tf_op jit(solution)/shard_map/psum | solution.py:188
  821.4 2.0 copy.21
  823.5 2.0 copy.22
  (178 shorter events, 4.3 us)
Async XLA Ops:
  7.2 330.5 %copy-start = (bf16[512,1024]{1,0:T(8,128)(2,1)S(1)}, bf16[512,1024]{1,0:T(8,128)(2,1)}, u32[]{:S(2)}) copy-start(bf16[512,1024]{1,0:T(8,128)(2,1)} %param.20) | copy-start | bytes 3145732
  7.2 6.6 copy-start.19
  7.2 6.5 copy-start.82
  7.2 6.6 copy-start.30
  7.2 6.6 copy-start.45
  7.2 163.2 %all-gather.3.cloned.1.call-start = ((), (), s32[]{:S(2)}) async-start(), calls=%async_computation.2 | async-start | bytes 4325376 | tf_op jit(solution)/shard_map/all_gather | solution.py:150
  9.4 320.5 %all-gather.5.cloned.1.call-start = ((), (), s32[]{:S(2)}) async-start(), calls=%async_computation.3 | async-start | bytes 4325376 | tf_op jit(solution)/shard_map/all_gather | solution.py:151
  11.5 515.4 %reduce-scatter.5.cloned.1.call-start = ((), (), s32[]{:S(2)}) async-start(), calls=%async_computation.5 | async-start | bytes 8650752 | tf_op jit(solution)/shard_map/reduce_scatter | solution.py:168
  12.6 161.6 %copy-start.47 = (f32[128]{0:T(128)}, f32[128]{0:T(128)S(1)}, u32[]{:S(2)}) copy-start(f32[128]{0:T(128)S(1)} %broadcast_multiply_fusion.3) | copy-start | bytes 1540
  13.7 160.4 %copy-start.62 = (f32[128]{0:T(128)}, f32[128]{0:T(128)S(1)}, u32[]{:S(2)}) copy-start(f32[128]{0:T(128)S(1)} %add_rsqrt_fusion.1) | copy-start | bytes 1540
  14.1 163.4 %copy-start.24 = (bf16[128,512]{1,0:T(8,128)(2,1)}, bf16[128,512]{1,0:T(8,128)(2,1)S(1)}, u32[]{:S(2)}) copy-start(bf16[128,512]{1,0:T(8,128)(2,1)S(1)} %convolution_convert_fusion.11) | copy-start | bytes 393220
  170.4 3.7 copy-start.11
  172.3 157.6 %copy-start.58 = (f32[128]{0:T(128)}, f32[128]{0:T(128)S(1)}, u32[]{:S(2)}) copy-start(f32[128]{0:T(128)S(1)} %get-tuple-element.35) | copy-start | bytes 1540
  174.1 155.8 %copy-start.73 = (f32[128]{0:T(128)}, f32[128]{0:T(128)S(1)}, u32[]{:S(2)}) copy-start(f32[128]{0:T(128)S(1)} %fusion.5) | copy-start | bytes 1540
  174.7 157.9 %copy-start.55 = (f32[128]{0:T(128)}, f32[128]{0:T(128)S(1)}, u32[]{:S(2)}) copy-start(f32[128]{0:T(128)S(1)} %get-tuple-element.33) | copy-start | bytes 1540
  176.4 156.2 %copy-start.70 = (f32[128]{0:T(128)}, f32[128]{0:T(128)S(1)}, u32[]{:S(2)}) copy-start(f32[128]{0:T(128)S(1)} %fusion.7) | copy-start | bytes 1540
  177.0 157.5 %copy-start.52 = (f32[128]{0:T(128)}, f32[128]{0:T(128)S(1)}, u32[]{:S(2)}) copy-start(f32[128]{0:T(128)S(1)} %get-tuple-element.31) | copy-start | bytes 1540
  177.5 157.0 %copy-start.67 = (f32[128]{0:T(128)}, f32[128]{0:T(128)S(1)}, u32[]{:S(2)}) copy-start(f32[128]{0:T(128)S(1)} %fusion.9) | copy-start | bytes 1540
  178.3 157.7 %copy-start.49 = (f32[128]{0:T(128)}, f32[128]{0:T(128)S(1)}, u32[]{:S(2)}) copy-start(f32[128]{0:T(128)S(1)} %get-tuple-element.29) | copy-start | bytes 1540
  178.7 157.3 %copy-start.64 = (f32[128]{0:T(128)}, f32[128]{0:T(128)S(1)}, u32[]{:S(2)}) copy-start(f32[128]{0:T(128)S(1)} %fusion.11) | copy-start | bytes 1540
  329.9 2.7 copy-start.6
  329.9 3.8 copy-start.78
  333.7 3.1 copy-start.36
  333.7 1.6 copy-start.3
  335.3 1.5 copy-start.38
  336.1 1.6 copy-start.44
  337.1 1.9 copy-start.42
  338.5 1.7 copy-start.21
  339.1 1.6 copy-start.56
  339.1 1.6 copy-start.71
  340.7 3.0 copy-start.34
  340.7 1.6 copy-start.9
  340.7 1.6 copy-start.59
  340.7 1.6 copy-start.74
  347.9 356.5 %reduce-scatter.3.cloned.1.call-start = ((), (), s32[]{:S(2)}) async-start(), calls=%async_computation.4 | async-start | bytes 8650752 | tf_op jit(solution)/shard_map/reduce_scatter | solution.py:167
  348.5 2.7 copy-start.10
  348.5 2.8 copy-start.61
  348.5 2.8 copy-start.76
  351.3 2.3 copy-start.79
  352.2 2.3 copy-start.7
  352.2 2.3 copy-start.57
  352.2 2.3 copy-start.72
  355.9 2.7 copy-start.13
  355.9 2.0 copy-start.4
  355.9 2.0 copy-start.54
  356.0 2.0 copy-start.69
  359.3 1.4 copy-start.15
  366.8 2.0 copy-start.14
  366.8 4.0 copy-start.16
  366.8 4.0 copy-start.12
  368.8 2.7 copy-start.18
  371.5 1.6 copy-start.29
  372.1 1.5 copy-start.27
  372.1 1.5 copy-start.37
  372.1 1.5 copy-start.39
  372.1 1.5 copy-start.41
  372.1 1.5 copy-start.43
  373.0 3.3 copy-start.22
  373.0 3.3 copy-start.33
  374.9 3.3 copy-start.81
  376.3 150.7 %copy-start.23 = (bf16[1,128,512]{2,1,0:T(8,128)(2,1)S(1)}, bf16[1,128,512]{2,1,0:T(8,128)(2,1)}, u32[]{:S(2)}) copy-start(bf16[1,128,512]{2,1,0:T(8,128)(2,1)} %param.13) | copy-start | bytes 393220
  378.1 328.8 %copy-start.46 = (f32[512]{0:T(512)S(1)}, f32[512]{0:T(512)}, u32[]{:S(2)}) copy-start(f32[512]{0:T(512)} %get-tuple-element.18) | copy-start | bytes 6148
  378.1 328.8 %copy-start.77 = (f32[512]{0:T(512)S(1)}, f32[512]{0:T(512)}, u32[]{:S(2)}) copy-start(f32[512]{0:T(512)} %fusion.14) | copy-start | bytes 6148
  707.0 118.6 %copy-start.1 = (bf16[512,1024]{1,0:T(8,128)(2,1)S(1)}, bf16[512,1024]{1,0:T(8,128)(2,1)}, u32[]{:S(2)}) copy-start(bf16[512,1024]{1,0:T(8,128)(2,1)} %param.20) | copy-start | bytes 3145732
  (23 other events, 22.6 us)
Sparse Core Ops, SparseCore 0:
  10.3 160.0 all-gather.2
  172.6 157.2 all-gather.4
  348.0 178.8 reduce-scatter.4
  529.2 175.1 reduce-scatter.2
where the time goes:
time: 833 us; the launch traced here: 832 us
  waiting for transfers between devices  630 us (76%)
  blocking collectives  114 us (14%)
  matrix products  41.7 us (5%)
  local copies, waits for them, and re-layouts  16 us (2%)
  between operations  14.7 us (2%)
  other arithmetic  14.5 us (2%)
    reduce_scatter x1, waiting for transfers between devices, local(): lax.psum_scatter(partial_keys.astype(jnp.float32), 'geom', scatter_dimens...  175 us
    all_gather x1, waiting for transfers between devices, local(): lax.all_gather(local_keys, 'geom', axis=0, tiled=True)  156 us
    all_gather x1, waiting for transfers between devices, local(): lax.all_gather(local_values, 'geom', axis=0, tiled=True)  151 us
    reduce_scatter x1, waiting for transfers between devices, local(): lax.psum_scatter(partial_values.astype(jnp.float32), 'geom', scatter_dime...  148 us
    psum x1, blocking collectives, local(): lax.psum((grad_query, grad_key, grad_value, grad_out, grad_up, grad_down,...  114 us
  transfers between devices with their start and end apart: 4, of which 4 were waited for; matrix products, arithmetic and copies ran while one was open for 5% of the time, Pallas kernels for 0%

commit v1 on v0

--- a/solution.py
+++ b/solution.py
@@ -186,17 +186,20 @@
     )
     grad_query, grad_out, grad_up, grad_down, grad_gain_attn, grad_gain_mlp = grads
     totals = lax.psum(
-        (
-            grad_query,
-            grad_key,
-            grad_value,
-            grad_out,
-            grad_up,
-            grad_down,
-            grad_gain_attn,
-            grad_gain_mlp,
+        lax.psum(
+            (
+                grad_query,
+                grad_key,
+                grad_value,
+                grad_out,
+                grad_up,
+                grad_down,
+                grad_gain_attn,
+                grad_gain_mlp,
+            ),
+            "geom",
         ),
-        ("room", "geom"),
+        "room",
     )
     summed = [piece.astype(jnp.bfloat16) for piece in totals]
     return (

time: 833 us -> 1210 us (1.45)
  waiting for transfers between devices: 630 us -> 889 us
  blocking collectives: 114 us -> 227 us
    psum x0 -> x1, waiting for transfers between devices: none -> 259 us  [local(): lax.psum((grad_query, grad_key, grad_value, grad_out, grad_up, grad_down,...]
    psum x0 -> x1, blocking collectives: none -> 148 us  [local(): lax.psum(lax.psum((grad_query, grad_key, grad_value, grad_out, grad_up, g...]
    psum x1, blocking collectives: 114 us -> 78.4 us  [local(): lax.psum((grad_query, grad_key, grad_value, grad_out, grad_up, grad_down,...]
  transfers between devices with their start and end apart: 4 -> 5, of which waited for: 4 -> 5; matrix products, arithmetic and copies ran while one was open for 5% -> 3% of each run, Pallas kernels for 0% -> 0%
where the time goes in v1:
time: 1210 us; the launch traced here: 1200 us
  waiting for transfers between devices  889 us (73%)
  blocking collectives  227 us (19%)
  matrix products  44.1 us (4%)
  local copies, waits for them, and re-layouts  15 us (1%)
  between operations  14.7 us (1%)
  other arithmetic  14.3 us (1%)
    psum x1, waiting for transfers between devices, local(): lax.psum((grad_query, grad_key, grad_value, grad_out, grad_up, grad_down,...  259 us
    reduce_scatter x1, waiting for transfers between devices, local(): lax.psum_scatter(partial_keys.astype(jnp.float32), 'geom', scatter_dimens...  175 us
    all_gather x1, waiting for transfers between devices, local(): lax.all_gather(local_keys, 'geom', axis=0, tiled=True)  156 us
    all_gather x1, waiting for transfers between devices, local(): lax.all_gather(local_values, 'geom', axis=0, tiled=True)  151 us
    psum x1, blocking collectives, local(): lax.psum(lax.psum((grad_query, grad_key, grad_value, grad_out, grad_up, g...  148 us
    reduce_scatter x1, waiting for transfers between devices, local(): lax.psum_scatter(partial_values.astype(jnp.float32), 'geom', scatter_dime...  147 us
    psum x1, blocking collectives, local(): lax.psum((grad_query, grad_key, grad_value, grad_out, grad_up, grad_down,...  78.4 us
  transfers between devices with their start and end apart: 5, of which 5 were waited for; matrix products, arithmetic and copies ran while one was open for 3% of the time, Pallas kernels for 0%

profile of v1, /device:TPU:0, one launch (start us, length us, event | category | flops | bytes accessed | tf_op | source)
XLA Modules:
  0.0 1204.1 jit_solution(13717035341030003930)
XLA Ops:
  7.3 2.1 convolution_convert_fusion.10
  9.5 2.0 convolution_convert_fusion.9
  11.5 1.0 convert_reduce_fusion
  12.6 1.1 fusion.54
  14.1 156.3 %all-gather.3.cloned.1.call-done = bf16[4096,512]{1,0:T(8,128)(2,1)} async-done(((bf16[128,512]{1,0:T(8,128)(2,1)}), bf16[4096,512]{1,0:T(8,128)(2,1)}) %all-gather.3.cloned.1.call-update) | async-done | bytes 4194320 | tf_op jit(solution)/shard_map/all_gather | solution.py:150
  170.4 1.9 fusion.99
  172.3 1.4 copy-done.8
  173.7 0.4 fusion.5
  174.2 0.6 fusion.98
  174.7 1.3 copy-done.5
  176.0 0.4 fusion.7
  176.5 0.5 fusion.97
  177.5 0.5 fusion.96
  178.8 151.1 %all-gather.5.cloned.1.call-done = bf16[4096,512]{1,0:T(8,128)(2,1)} async-done(((bf16[128,512]{1,0:T(8,128)(2,1)}), bf16[4096,512]{1,0:T(8,128)(2,1)}) %all-gather.5.cloned.1.call-update) | async-done | bytes 4194320 | tf_op jit(solution)/shard_map/all_gather | solution.py:151
  329.9 2.7 convolution_convert_fusion.19
  332.7 1.0 copy-done.77
  333.7 0.7 convolution_convert_fusion.18
  334.5 0.8 copy-done.3
  335.3 0.7 convolution_convert_fusion.17
  336.1 0.7 convolution_convert_fusion.16
  338.5 0.6 fusion.12
  339.1 0.6 multiply_reduce_fusion.4
  340.3 0.6 convolution_convert_fusion.2
  340.9 1.0 copy-done.9
  341.9 0.6 convolution_convert_fusion.3
  342.6 0.6 convolution_convert_fusion.1
  343.2 0.6 convolution_convert_fusion
  343.8 3.6 maximum_convert_fusion.1
  348.1 2.7 multiply_reduce_fusion.3
  350.9 0.7 multiply_convert_fusion.3
  351.8 0.5 convolution_convert_fusion.7
  352.3 0.9 copy-done.78
  353.2 0.9 copy-done.7
  354.1 0.7 multiply_reduce_fusion.2
  354.7 0.7 multiply_convert_fusion.2
  355.5 0.5 convolution_convert_fusion.6
  356.0 1.5 copy-done.4
  357.5 0.7 multiply_reduce_fusion.1
  358.1 0.7 multiply_convert_fusion.1
  358.9 0.5 convolution_convert_fusion.5
  359.6 0.7 multiply_reduce_fusion
  360.3 0.7 multiply_convert_fusion
  361.0 1.0 copy-done.17
  362.0 0.5 convolution_convert_fusion.4
  362.5 3.7 maximum_convert_fusion
  366.2 2.4 fusion.79
  368.6 1.9 convolution_convert_fusion.15
  370.6 1.8 convolution_convert_fusion.14
  372.5 0.6 convolution_convert_fusion.13
  373.1 0.6 convolution_convert_fusion.12
  373.7 1.4 fusion.78
  375.1 1.9 fusion.86
  377.0 1.8 fusion.55
  378.8 147.3 %reduce-scatter.5.cloned.1.call-done = f32[128,512]{1,0:T(8,128)} async-done(((f32[4096,512]{1,0:T(8,128)}), f32[128,512]{1,0:T(8,128)}) %reduce-scatter.5.cloned.1.call-update) | async-done | bytes 262160 | tf_op jit(solution)/shard_map/reduce_scatter | solution.py:168
  526.0 2.6 convolution_bitcast_fusion
  528.7 175.2 %reduce-scatter.3.cloned.1.call-done = f32[128,512]{1,0:T(8,128)} async-done(((f32[4096,512]{1,0:T(8,128)}), f32[128,512]{1,0:T(8,128)}) %reduce-scatter.3.cloned.1.call-update) | async-done | bytes 262160 | tf_op jit(solution)/shard_map/reduce_scatter | solution.py:167
  703.9 2.5 convolution_bitcast_fusion.1
  706.5 1.0 copy-done.30
  707.8 78.4 %all-reduce = (f32[512]{0:T(512)S(1)}, f32[512]{0:T(512)S(1)}) all-reduce(f32[512]{0:T(512)S(1)} %fusion.14, f32[512]{0:T(512)S(1)} %get-tuple-element.18), channel_id=1, replica_groups=mesh['room'=4,'geom'=32] {'geom'}, use_global_device_ids=true, to_apply=%region_33.34 | all-reduce | flops 1024 | bytes 8192 | tf_op jit(solution)/shard_map/psum | solution.py:189
  786.2 2.2 fusion.15
  788.5 259.0 %all-reduce.6.cloned.1.call-done = (f32[512,512]{1,0:T(8,128)}, f32[512,512]{0,1:T(8,128)}, f32[512,512]{0,1:T(8,128)}, f32[512,512]{1,0:T(8,128)}, f32[512,1024]{1,0:T(8,128)}, /*index=5*/f32[1024,512]{1,0:T(8,128)}) async-done(((f32[512,512]{1,0:T(8,128)}, f32[512,512]{0,1:T(8,128)}, f32[512,512]{0,1:T(8,128)}, f32[512,512]{1,0:T(8,128)}, f32[512,1024]{1,0:T(8,128)}, /*index=5*/f32[1024,512]{1,0:T(8,128)}), ...) | async-done | bytes 8388624 | tf_op jit(solution)/shard_map/psum | solution.py:189
  1047.5 148.1 %all-reduce.7 = (bf16[512,512]{1,0:T(8,128)(2,1)}, bf16[512,512]{0,1:T(8,128)(2,1)S(1)}, bf16[512,512]{0,1:T(8,128)(2,1)S(1)}, bf16[512,512]{1,0:T(8,128)(2,1)},...) all-reduce(f32[512,512]{1,0:T(8,128)} %get-tuple-element.23, ...), channel_id=1, replica_groups=mesh['room'=4,'geom'=32] {'room'}, use_global_device_ids=true, to_apply=%region_19.20 | all-reduce | flops 2098176 | bytes 12589056 | tf_op jit(solution)/shard_map/psum | solution.py:188
  1195.6 1.0 copy.21
  1196.6 1.0 copy.22
  (178 shorter events, 5.5 us)
Async XLA Ops:
  7.2 330.5 %copy-start = (bf16[512,1024]{1,0:T(8,128)(2,1)S(1)}, bf16[512,1024]{1,0:T(8,128)(2,1)}, u32[]{:S(2)}) copy-start(bf16[512,1024]{1,0:T(8,128)(2,1)} %param.20) | copy-start | bytes 3145732
  7.2 6.6 copy-start.19
  7.2 6.5 copy-start.80
  7.2 6.6 copy-start.29
  7.2 6.6 copy-start.44
  7.2 163.2 %all-gather.3.cloned.1.call-start = ((), (), s32[]{:S(2)}) async-start(), calls=%async_computation.2 | async-start | bytes 4325376 | tf_op jit(solution)/shard_map/all_gather | solution.py:150
  9.4 320.5 %all-gather.5.cloned.1.call-start = ((), (), s32[]{:S(2)}) async-start(), calls=%async_computation.3 | async-start | bytes 4325376 | tf_op jit(solution)/shard_map/all_gather | solution.py:151
  11.5 514.5 %reduce-scatter.5.cloned.1.call-start = ((), (), s32[]{:S(2)}) async-start(), calls=%async_computation.5 | async-start | bytes 8650752 | tf_op jit(solution)/shard_map/reduce_scatter | solution.py:168
  12.6 161.6 %copy-start.47 = (f32[128]{0:T(128)}, f32[128]{0:T(128)S(1)}, u32[]{:S(2)}) copy-start(f32[128]{0:T(128)S(1)} %broadcast_multiply_fusion.3) | copy-start | bytes 1540
  13.7 158.6 %copy-start.62 = (f32[128]{0:T(128)}, f32[128]{0:T(128)S(1)}, u32[]{:S(2)}) copy-start(f32[128]{0:T(128)S(1)} %add_rsqrt_fusion.1) | copy-start | bytes 1540
  14.1 163.4 %copy-start.24 = (bf16[128,512]{1,0:T(8,128)(2,1)}, bf16[128,512]{1,0:T(8,128)(2,1)S(1)}, u32[]{:S(2)}) copy-start(bf16[128,512]{1,0:T(8,128)(2,1)S(1)} %convolution_convert_fusion.11) | copy-start | bytes 393220
  170.4 3.7 copy-start.11
  172.3 1.4 copy-start.8
  172.3 157.6 %copy-start.58 = (f32[128]{0:T(128)}, f32[128]{0:T(128)S(1)}, u32[]{:S(2)}) copy-start(f32[128]{0:T(128)S(1)} %get-tuple-element.43) | copy-start | bytes 1540
  174.1 155.8 %copy-start.73 = (f32[128]{0:T(128)}, f32[128]{0:T(128)S(1)}, u32[]{:S(2)}) copy-start(f32[128]{0:T(128)S(1)} %fusion.5) | copy-start | bytes 1540
  174.7 1.3 copy-start.5
  174.7 157.9 %copy-start.55 = (f32[128]{0:T(128)}, f32[128]{0:T(128)S(1)}, u32[]{:S(2)}) copy-start(f32[128]{0:T(128)S(1)} %get-tuple-element.41) | copy-start | bytes 1540
  176.4 156.2 %copy-start.70 = (f32[128]{0:T(128)}, f32[128]{0:T(128)S(1)}, u32[]{:S(2)}) copy-start(f32[128]{0:T(128)S(1)} %fusion.7) | copy-start | bytes 1540
  177.0 1.3 copy-start.2
  177.0 157.4 %copy-start.52 = (f32[128]{0:T(128)}, f32[128]{0:T(128)S(1)}, u32[]{:S(2)}) copy-start(f32[128]{0:T(128)S(1)} %get-tuple-element.39) | copy-start | bytes 1540
  177.5 157.0 %copy-start.67 = (f32[128]{0:T(128)}, f32[128]{0:T(128)S(1)}, u32[]{:S(2)}) copy-start(f32[128]{0:T(128)S(1)} %fusion.9) | copy-start | bytes 1540
  178.3 157.7 %copy-start.49 = (f32[128]{0:T(128)}, f32[128]{0:T(128)S(1)}, u32[]{:S(2)}) copy-start(f32[128]{0:T(128)S(1)} %get-tuple-element.37) | copy-start | bytes 1540
  178.8 157.3 %copy-start.64 = (f32[128]{0:T(128)}, f32[128]{0:T(128)S(1)}, u32[]{:S(2)}) copy-start(f32[128]{0:T(128)S(1)} %fusion.11) | copy-start | bytes 1540
  329.9 2.7 copy-start.6
  329.9 3.8 copy-start.77
  333.7 3.1 copy-start.39
  333.7 1.6 copy-start.3
  335.3 1.5 copy-start.40
  336.1 1.6 copy-start.43
  337.1 1.9 copy-start.42
  337.1 1.3 copy-start.79
  337.7 2.0 copy-start.45
  338.5 1.2 copy-start.21
  340.2 3.0 copy-start.37
  340.2 1.6 copy-start.9
  340.2 1.6 copy-start.59
  340.2 1.6 copy-start.74
  347.4 356.4 %reduce-scatter.3.cloned.1.call-start = ((), (), s32[]{:S(2)}) async-start(), calls=%async_computation.4 | async-start | bytes 8650752 | tf_op jit(solution)/shard_map/reduce_scatter | solution.py:167
  348.1 2.7 copy-start.10
  348.1 2.8 copy-start.61
  348.1 2.8 copy-start.76
  350.9 1.4 copy-start.38
  350.9 2.3 copy-start.78
  351.8 2.3 copy-start.7
  351.8 2.3 copy-start.57
  351.8 2.3 copy-start.72
  355.5 2.7 copy-start.13
  355.5 2.0 copy-start.4
  355.5 2.0 copy-start.54
  355.5 2.0 copy-start.69
  358.9 1.4 copy-start.15
  366.1 6.3 copy-start.16
  366.2 4.4 copy-start.14
  366.2 681.3 %all-reduce.6.cloned.1.call-start = ((), (), s32[]{:S(2)}) async-start(), calls=%async_computation.6 | async-start | bytes 16777216 | tf_op jit(solution)/shard_map/psum | solution.py:189
  368.6 3.8 copy-start.12
  370.6 3.1 copy-start.33
  370.6 2.5 copy-start.18
  372.4 1.2 copy-start.35
  373.0 2.0 copy-start.28
  373.1 2.0 copy-start.46
  373.7 3.3 copy-start.22
  373.7 3.3 copy-start.32
  375.1 151.0 %copy-start.23 = (bf16[1,128,512]{2,1,0:T(8,128)(2,1)S(1)}, bf16[1,128,512]{2,1,0:T(8,128)(2,1)}, u32[]{:S(2)}) copy-start(bf16[1,128,512]{2,1,0:T(8,128)(2,1)} %param.13) | copy-start | bytes 393220
  1047.5 150.1 %copy-start.1 = (bf16[512,1024]{1,0:T(8,128)(2,1)S(1)}, bf16[512,1024]{1,0:T(8,128)(2,1)}, u32[]{:S(2)}) copy-start(bf16[512,1024]{1,0:T(8,128)(2,1)} %param.20) | copy-start | bytes 3145732
  (22 other events, 19.8 us)
Sparse Core Ops, SparseCore 0:
  10.3 160.0 all-gather.2
  172.6 157.2 all-gather.4
  347.6 178.4 reduce-scatter.4
  528.3 175.5 reduce-scatter.2
  707.3 340.1 all-reduce.5
